TPU v7x, 768 devices: a whole 4x8x12 slice. The times are simulated.
768 devices in a mesh: dp: 48 (over x, z), pipe: 8 (over y_lo, core), mp: 2 (over y_hi).
Axes of the slice: x: 4, y: 8 (y_hi: 2, y_lo: 4; y = y_hi * 4 + y_lo), z: 12, core: 2. Of those that a mesh axis runs over, the one named last changes fastest.
Arguments:
- latents: bfloat16 [48, 2, 64, 3072], P('dp'), may hold values from -6 to 6
- caption_kv: bfloat16 [48, 8, 2, 128, 1536], P('dp', 'pipe', None, None, 'mp'), may hold values from -6 to 6
- caption_mask: int32 [48, 128], P('dp'), may hold values from 0 to 1, as said below
- query_weight: bfloat16 [8, 3072, 1536], P('pipe', None, 'mp'), may hold values from -0.109375 to 0.109375
- out_weight: bfloat16 [8, 1536, 3072], P('pipe', 'mp'), may hold values from -0.15625 to 0.15625
- gate: float32 [8, 3072], P('pipe'), may hold values from 0.5 to 1.5
- cotangent: bfloat16 [48, 2, 64, 3072], P('dp'), may hold values from -6 to 6
Outputs:
- section_out: bfloat16 [8, 48, 2, 64, 3072], P('pipe', 'dp', None, None, 'mp')
- input_grad: bfloat16 [8, 48, 2, 64, 3072], P('pipe', 'dp', None, None, 'mp')
- out_weight_grad: float32 [8, 1536, 3072], P('pipe', 'mp', 'dp')
Inputs may be any that keep to these rules, and one draw needn't show every extreme that they name: `caption_mask`: each row is a run of ones followed by zeros; the first 32 entries of every row are 1, and some row is all ones.
All inputs are finite; a program needn't handle non-finite values.
Results may differ from a plain program's by a relative error of at most 0.04.
Values may be sent and summed in bfloat16 or wider, within the bound.
No kernel may reach another device: no remote copies, remote signals or barrier semaphores. Data moves between devices by JAX's collectives and lax.ppermute only.
A program may use at most 64 MiB of HBM per device.

v0:
```python
import math

import jax
import jax.numpy as jnp
from jax import lax
from jax.sharding import PartitionSpec as P

HEAD_DIM = 128


def from_everyone(value, axis):
    size = lax.axis_size(axis)
    return lax.all_to_all(
        jnp.broadcast_to(value[None], (size, *value.shape)), axis, 0, 0, tiled=True
    )


def over_copies(value, axis):
    everything = from_everyone(value, axis)
    return jnp.sum(everything.astype(jnp.float32), axis=0)


def from_behind(value, axis, steps):
    count = lax.axis_size(axis)
    leading, last = (max(0, -steps), min(count, count - steps))
    return lax.ppermute(value, axis, [(source, source + steps) for source in range(leading, last)])


def forward_parts(x_rows, w_query, kv_pair, live):
    rows = x_rows.shape[0]
    x_float = x_rows.astype(jnp.float32)
    scale_r = lax.rsqrt(jnp.mean(x_float * x_float, axis=-1, keepdims=True) + 1e-06)
    normed = (x_float * scale_r).astype(jnp.bfloat16)
    query = jnp.dot(normed, w_query, preferred_element_type=jnp.float32).astype(jnp.bfloat16)
    q_heads = query.reshape(rows, -1, HEAD_DIM).astype(jnp.float32)
    k_heads = kv_pair[0].reshape(kv_pair.shape[1], -1, HEAD_DIM).astype(jnp.float32)
    v_heads = kv_pair[1].reshape(kv_pair.shape[1], -1, HEAD_DIM).astype(jnp.float32)
    scores = jnp.einsum("rhd,chd->hrc", q_heads, k_heads) / math.sqrt(HEAD_DIM)
    scores = jnp.where(live[None, None, :] > 0, scores, -1e30)
    prob = jax.nn.softmax(scores, axis=-1)
    probs = lax.optimization_barrier(prob.astype(jnp.bfloat16)).astype(jnp.float32)
    attended = jnp.einsum("hrc,chd->rhd", probs, v_heads).reshape(rows, -1).astype(jnp.bfloat16)
    return (x_float, scale_r, prob, attended, k_heads, v_heads)


def forward_local(x_rows, w_query, w_out, kv_pair, live):
    parts = forward_parts(x_rows, w_query, kv_pair, live)
    return jnp.dot(parts[3], w_out, preferred_element_type=jnp.float32)


def backward_local(x_rows, grad_rows, w_query, w_out, kv_pair, live, gain):
    rows = x_rows.shape[0]
    x_float, scale_r, prob, attended, k_heads, v_heads = forward_parts(
        x_rows, w_query, kv_pair, live
    )
    dproj = (gain * grad_rows.astype(jnp.float32)).astype(jnp.bfloat16)
    dattended = jnp.dot(dproj, w_out.T, preferred_element_type=jnp.float32).astype(jnp.bfloat16)
    d_heads = dattended.reshape(rows, -1, HEAD_DIM).astype(jnp.float32)
    dprob = jnp.einsum("rhd,chd->hrc", d_heads, v_heads)
    dscore = (prob * (dprob - jnp.sum(prob * dprob, axis=-1, keepdims=True))).astype(jnp.bfloat16)
    dscore_f = lax.optimization_barrier(dscore).astype(jnp.float32)
    dquery = (
        (jnp.einsum("hrc,chd->rhd", dscore_f, k_heads) / math.sqrt(HEAD_DIM))
        .reshape(rows, -1)
        .astype(jnp.bfloat16)
    )
    partial_dn = jnp.dot(dquery, w_query.T, preferred_element_type=jnp.float32)
    return (partial_dn, attended, dproj)


def per_device(latents, caption_kv, caption_mask, query_weight, out_weight, gate, cotangent):
    micro, tok, width = (latents.shape[1], latents.shape[2], latents.shape[3])
    rows = micro * tok
    w_query = query_weight[0]
    w_out = out_weight[0]
    kv_pair = caption_kv[0, 0]
    live = caption_mask[0]
    gain = gate[0]
    inner_width = w_out.shape[0]
    sections = lax.axis_size("pipe")
    position = lax.axis_index("pipe")
    share = width // lax.axis_size("mp")
    offset = lax.axis_index("mp") * share

    def own_part(values):
        return lax.dynamic_slice_in_dim(values, offset, share, 1)

    def forward_busy(x_rows):
        return forward_local(x_rows, w_query, w_out, kv_pair, live)

    def forward_quiet(x_rows):
        return jnp.zeros((rows, width), jnp.float32)

    def forward_turn(step, carry):
        current, saved, result = carry
        mine = position == step
        partial_proj = lax.cond(mine, forward_busy, forward_quiet, current)
        x_now = current.astype(jnp.float32)
        proj = over_copies(partial_proj.astype(jnp.bfloat16), "mp").astype(jnp.float32)
        output = (x_now + gain * proj).astype(jnp.bfloat16)
        output_share = own_part(output)
        arrived = from_behind(output, "pipe", 1)
        saved = jnp.where(mine, current, saved)
        result = jnp.where(mine, output_share, result)
        current = jnp.where(position == step + 1, arrived, current)
        return (current, saved, result)

    start = latents.reshape(rows, width)
    _, saved, result = lax.fori_loop(0, sections, forward_turn, (start, start, own_part(start)))

    def backward_busy(operands):
        return backward_local(operands[0], operands[1], w_query, w_out, kv_pair, live, gain)

    def backward_quiet(operands):
        return (
            jnp.zeros((rows, width), jnp.float32),
            jnp.zeros((rows, inner_width), jnp.bfloat16),
            jnp.zeros((rows, width), jnp.bfloat16),
        )

    x_float = saved.astype(jnp.float32)
    scale_r = lax.rsqrt(jnp.mean(x_float * x_float, axis=-1, keepdims=True) + 1e-06)

    def backward_turn(count, carry):
        incoming, grad_in, attended, dproj = carry
        active = sections - 1 - count
        mine = position == active
        partial_dn, attended_now, dproj_now = lax.cond(
            mine, backward_busy, backward_quiet, (saved, incoming)
        )
        dnormed = over_copies(partial_dn.astype(jnp.bfloat16), "mp").astype(jnp.float32)
        inner = jnp.mean(dnormed * x_float, axis=-1, keepdims=True)
        dx = (
            incoming.astype(jnp.float32)
            + scale_r * (dnormed - x_float * (scale_r * scale_r) * inner)
        ).astype(jnp.bfloat16)
        dx_share = own_part(dx)
        arrived = from_behind(dx, "pipe", -1)
        grad_in = jnp.where(mine, dx_share, grad_in)
        attended = jnp.where(mine, attended_now, attended)
        dproj = jnp.where(mine, dproj_now, dproj)
        incoming = jnp.where(position == active - 1, arrived, incoming)
        return (incoming, grad_in, attended, dproj)

    incoming0 = cotangent.reshape(rows, width)
    init = (
        incoming0,
        own_part(incoming0),
        jnp.zeros((rows, inner_width), jnp.bfloat16),
        jnp.zeros((rows, width), jnp.bfloat16),
    )
    _, grad_in, attended, dproj = lax.fori_loop(0, sections, backward_turn, init)
    columns = lax.all_to_all(dproj, "dp", split_axis=1, concat_axis=0, tiled=True)
    weight_grad = lax.dot_general(
        lax.all_gather(attended, "dp", axis=0, tiled=True),
        columns,
        (((0,), (0,)), ((), ())),
        preferred_element_type=jnp.float32,
    )
    section_out = result.reshape(1, 1, micro, tok, share)
    input_grad = grad_in.reshape(1, 1, micro, tok, share)
    return (section_out, input_grad, weight_grad[None])


def solution(mesh):
    return jax.shard_map(
        per_device,
        mesh=mesh,
        in_specs=(
            P("dp", None, None, None),
            P("dp", "pipe", None, None, "mp"),
            P("dp", None),
            P("pipe", None, "mp"),
            P("pipe", "mp", None),
            P("pipe", None),
            P("dp", None, None, None),
        ),
        out_specs=(
            P("pipe", "dp", None, None, "mp"),
            P("pipe", "dp", None, None, "mp"),
            P("pipe", "mp", "dp"),
        ),
        check_vma=False,
    )
```

profile of v0, /device:TPU:16, one launch (start us, length us, event | category | flops | bytes accessed | tf_op | source)
XLA Modules:
  0.0 1174.9 jit_solution(8187409583302420944)
XLA Ops:
  10.7 448.7 %while.43 = (s32[]{:T(128)}, bf16[128,3072]{1,0:T(8,128)(2,1)S(1)}, bf16[128,3072]{1,0:T(8,128)(2,1)S(1)}, bf16[128,1536]{1,0:T(8,128)(2,1)}, s32[]{:T(128)}, /*...) while((s32[]{:T(128)}, bf16[128,3072]{1,0:T(8,128)(2,1)S(1)}, ...), condition=%wide.region_7.8_spmd, body=%wide.region_0.7_spmd.sunk | while | flops 1265172864 | bytes 35410924 | solution.py:109
  11.0 39.2 %all_to_all.49 = bf16[2,128,3072]{2,1,0:T(8,128)(2,1)S(1)} all-to-all(bf16[2,128,3072]{2,1,0:T(8,128)(2,1)S(1)} %broadcast_in_dim.98), channel_id=1, replica_groups=mesh['dp'=48,'pipe'=8,'mp'=2] {'mp'}, dimensions={0} | all-to-all | bytes 3145728 | tf_op jit(solution)/shard_map/while/body/eval_jaxpr/all_to_all | solution.py:13
  70.4 28.5 %all_to_all.49 = bf16[2,128,3072]{2,1,0:T(8,128)(2,1)S(1)} all-to-all(bf16[2,128,3072]{2,1,0:T(8,128)(2,1)S(1)} %broadcast_in_dim.98), channel_id=1, replica_groups=mesh['dp'=48,'pipe'=8,'mp'=2] {'mp'}, dimensions={0} | all-to-all | bytes 3145728 | tf_op jit(solution)/shard_map/while/body/eval_jaxpr/all_to_all | solution.py:13
  116.4 43.5 %all_to_all.49 = bf16[2,128,3072]{2,1,0:T(8,128)(2,1)S(1)} all-to-all(bf16[2,128,3072]{2,1,0:T(8,128)(2,1)S(1)} %broadcast_in_dim.98), channel_id=1, replica_groups=mesh['dp'=48,'pipe'=8,'mp'=2] {'mp'}, dimensions={0} | all-to-all | bytes 3145728 | tf_op jit(solution)/shard_map/while/body/eval_jaxpr/all_to_all | solution.py:13
  164.2 26.6 %collective-permute-done = bf16[128,3072]{1,0:T(8,128)(2,1)} collective-permute-done((bf16[128,3072]{1,0:T(8,128)(2,1)S(1)}, bf16[128,3072]{1,0:T(8,128)(2,1)}, u32[]{:S(2)}, u32[]{:S(2)}) %collective-permute-start) | collective-permute-done | bytes 786464 | tf_op jit(solution)/shard_map/while/body/eval_jaxpr/ppermute | solution.py:26
  191.5 20.6 %all_to_all.49 = bf16[2,128,3072]{2,1,0:T(8,128)(2,1)S(1)} all-to-all(bf16[2,128,3072]{2,1,0:T(8,128)(2,1)S(1)} %broadcast_in_dim.98), channel_id=1, replica_groups=mesh['dp'=48,'pipe'=8,'mp'=2] {'mp'}, dimensions={0} | all-to-all | bytes 3145728 | tf_op jit(solution)/shard_map/while/body/eval_jaxpr/all_to_all | solution.py:13
  216.4 40.2 %collective-permute-done = bf16[128,3072]{1,0:T(8,128)(2,1)} collective-permute-done((bf16[128,3072]{1,0:T(8,128)(2,1)S(1)}, bf16[128,3072]{1,0:T(8,128)(2,1)}, u32[]{:S(2)}, u32[]{:S(2)}) %collective-permute-start) | collective-permute-done | bytes 786464 | tf_op jit(solution)/shard_map/while/body/eval_jaxpr/ppermute | solution.py:26
  268.5 19.8 %all_to_all.49 = bf16[2,128,3072]{2,1,0:T(8,128)(2,1)S(1)} all-to-all(bf16[2,128,3072]{2,1,0:T(8,128)(2,1)S(1)} %broadcast_in_dim.98), channel_id=1, replica_groups=mesh['dp'=48,'pipe'=8,'mp'=2] {'mp'}, dimensions={0} | all-to-all | bytes 3145728 | tf_op jit(solution)/shard_map/while/body/eval_jaxpr/all_to_all | solution.py:13
  303.9 31.6 %all_to_all.49 = bf16[2,128,3072]{2,1,0:T(8,128)(2,1)S(1)} all-to-all(bf16[2,128,3072]{2,1,0:T(8,128)(2,1)S(1)} %broadcast_in_dim.98), channel_id=1, replica_groups=mesh['dp'=48,'pipe'=8,'mp'=2] {'mp'}, dimensions={0} | all-to-all | bytes 3145728 | tf_op jit(solution)/shard_map/while/body/eval_jaxpr/all_to_all | solution.py:13
  358.6 25.7 %all_to_all.49 = bf16[2,128,3072]{2,1,0:T(8,128)(2,1)S(1)} all-to-all(bf16[2,128,3072]{2,1,0:T(8,128)(2,1)S(1)} %broadcast_in_dim.98), channel_id=1, replica_groups=mesh['dp'=48,'pipe'=8,'mp'=2] {'mp'}, dimensions={0} | all-to-all | bytes 3145728 | tf_op jit(solution)/shard_map/while/body/eval_jaxpr/all_to_all | solution.py:13
  388.7 22.6 %collective-permute-done = bf16[128,3072]{1,0:T(8,128)(2,1)} collective-permute-done((bf16[128,3072]{1,0:T(8,128)(2,1)S(1)}, bf16[128,3072]{1,0:T(8,128)(2,1)}, u32[]{:S(2)}, u32[]{:S(2)}) %collective-permute-start) | collective-permute-done | bytes 786464 | tf_op jit(solution)/shard_map/while/body/eval_jaxpr/ppermute | solution.py:26
  412.0 26.7 %all_to_all.49 = bf16[2,128,3072]{2,1,0:T(8,128)(2,1)S(1)} all-to-all(bf16[2,128,3072]{2,1,0:T(8,128)(2,1)S(1)} %broadcast_in_dim.98), channel_id=1, replica_groups=mesh['dp'=48,'pipe'=8,'mp'=2] {'mp'}, dimensions={0} | all-to-all | bytes 3145728 | tf_op jit(solution)/shard_map/while/body/eval_jaxpr/all_to_all | solution.py:13
  460.9 512.4 %while.44 = (s32[]{:T(128)}, bf16[128,3072]{1,0:T(8,128)(2,1)S(1)}, bf16[128,1536]{1,0:T(8,128)(2,1)}, bf16[128,768]{0,1:T(8,128)(2,1)}, bf16[128,3072]{1,0:T(8,...) while((s32[]{:T(128)}, bf16[128,3072]{1,0:T(8,128)(2,1)S(1)}, ...), condition=%wide.region_18.19_spmd.clone, body=%wide.region_9.18_spmd.clone.sunk | while | flops 1949271296 | bytes 54689016 | solution.py:152
  470.7 22.8 %all-to-all-done.1 = bf16[2,128,3072]{2,1,0:T(8,128)(2,1)} async-done(((bf16[2,128,3072]{2,1,0:T(8,128)(2,1)}), bf16[2,128,3072]{2,1,0:T(8,128)(2,1)}, u32[]{:S(2)}, u32[]{:S(2)}) %all-to-all-start.1) | async-done | bytes 1572896 | tf_op jit(solution)/shard_map/while/body/eval_jaxpr/all_to_all | solution.py:13
  581.3 24.6 %all-to-all-done.1 = bf16[2,128,3072]{2,1,0:T(8,128)(2,1)} async-done(((bf16[2,128,3072]{2,1,0:T(8,128)(2,1)}), bf16[2,128,3072]{2,1,0:T(8,128)(2,1)}, u32[]{:S(2)}, u32[]{:S(2)}) %all-to-all-start.1) | async-done | bytes 1572896 | tf_op jit(solution)/shard_map/while/body/eval_jaxpr/all_to_all | solution.py:13
  609.8 19.3 %collective-permute-start.1 = (bf16[128,3072]{1,0:T(8,128)(2,1)}, bf16[128,3072]{1,0:T(8,128)(2,1)}, u32[]{:S(2)}, u32[]{:S(2)}) collective-permute-start(bf16[128,3072]{1,0:T(8,128)(2,1)} %add_convert_fusion.5), channel_id=1, source_target_pairs={{2,0},{4,2},{6,4},{8,6},{10,8},{12,10},{14,12},{3,1},{5,3},{7,5},{... | collective-permute-start | bytes 2359304 | tf_op jit(solution)/shard_map/while/body/eval_jaxpr/ppermute | solution.py:26
  649.8 27.1 %conditional.6 = (bf16[128,3072]{1,0:T(8,128)(2,1)}, bf16[128,768]{0,1:T(8,128)(2,1)}, bf16[128,3072]{1,0:T(8,128)(2,1)}) conditional(s32[]{:T(128)} %convert_element_type.243, () %tuple.114, (s32[1,128]{1,0:T(1,128)}, bf16[128,3072]{1,0:T(8,128)(2,1)S(1)}, bf16[3072,768]{1,0:T(8,128)(2,1)}, bf16[2,128,768]{1,2,0:T(8,128)(2,1)S(1)}, ...), branch_computations={%region_10.10_spmd, %region_11.15_spmd} | conditional | flops 1942979840 | bytes 26959696 | solution.py:128
  734.9 37.5 %all-to-all-done.1 = bf16[2,128,3072]{2,1,0:T(8,128)(2,1)} async-done(((bf16[2,128,3072]{2,1,0:T(8,128)(2,1)}), bf16[2,128,3072]{2,1,0:T(8,128)(2,1)}, u32[]{:S(2)}, u32[]{:S(2)}) %all-to-all-start.1) | async-done | bytes 1572896 | tf_op jit(solution)/shard_map/while/body/eval_jaxpr/all_to_all | solution.py:13
  804.6 19.6 %all-to-all-done.1 = bf16[2,128,3072]{2,1,0:T(8,128)(2,1)} async-done(((bf16[2,128,3072]{2,1,0:T(8,128)(2,1)}), bf16[2,128,3072]{2,1,0:T(8,128)(2,1)}, u32[]{:S(2)}, u32[]{:S(2)}) %all-to-all-start.1) | async-done | bytes 1572896 | tf_op jit(solution)/shard_map/while/body/eval_jaxpr/all_to_all | solution.py:13
  854.9 19.7 %all-to-all-done.1 = bf16[2,128,3072]{2,1,0:T(8,128)(2,1)} async-done(((bf16[2,128,3072]{2,1,0:T(8,128)(2,1)}), bf16[2,128,3072]{2,1,0:T(8,128)(2,1)}, u32[]{:S(2)}, u32[]{:S(2)}) %all-to-all-start.1) | async-done | bytes 1572896 | tf_op jit(solution)/shard_map/while/body/eval_jaxpr/all_to_all | solution.py:13
  878.5 25.9 %collective-permute-start.1 = (bf16[128,3072]{1,0:T(8,128)(2,1)}, bf16[128,3072]{1,0:T(8,128)(2,1)}, u32[]{:S(2)}, u32[]{:S(2)}) collective-permute-start(bf16[128,3072]{1,0:T(8,128)(2,1)} %add_convert_fusion.5), channel_id=1, source_target_pairs={{2,0},{4,2},{6,4},{8,6},{10,8},{12,10},{14,12},{3,1},{5,3},{7,5},{... | collective-permute-start | bytes 2359304 | tf_op jit(solution)/shard_map/while/body/eval_jaxpr/ppermute | solution.py:26
  924.3 23.6 %all-to-all-done.1 = bf16[2,128,3072]{2,1,0:T(8,128)(2,1)} async-done(((bf16[2,128,3072]{2,1,0:T(8,128)(2,1)}), bf16[2,128,3072]{2,1,0:T(8,128)(2,1)}, u32[]{:S(2)}, u32[]{:S(2)}) %all-to-all-start.1) | async-done | bytes 1572896 | tf_op jit(solution)/shard_map/while/body/eval_jaxpr/all_to_all | solution.py:13
  974.9 60.1 %all_to_all.48 = bf16[128,48,64]{0,2,1:T(8,128)(2,1)S(1)} all-to-all(bf16[128,48,64]{0,2,1:T(8,128)(2,1)S(1)} %bitcast.96), channel_id=1, replica_groups=mesh['dp'=48,'pipe'=8,'mp'=2] {'dp'}, dimensions={1} | all-to-all | bytes 1572864 | tf_op jit(solution)/shard_map/all_to_all | solution.py:153
  1035.0 125.7 %all-gather.2.cloned.1.call-done = bf16[6144,768]{0,1:T(8,128)(2,1)} async-done(((bf16[128,768]{0,1:T(8,128)(2,1)}), bf16[6144,768]{0,1:T(8,128)(2,1)}) %all-gather.2.cloned.1.call-update) | async-done | bytes 9437200 | tf_op jit(solution)/shard_map/all_gather | solution.py:155
  (273 shorter events, 484.9 us)
Async XLA Ops:
  7.2 1153.5 %all-gather.2.cloned.1.call-start = ((), (), s32[]{:S(2)}) async-start(), calls=%async_computation.3 | async-start | bytes 9633792 | tf_op jit(solution)/shard_map/all_gather | solution.py:155
  50.7 19.0 %collective-permute-start = (bf16[128,3072]{1,0:T(8,128)(2,1)S(1)}, bf16[128,3072]{1,0:T(8,128)(2,1)}, u32[]{:S(2)}, u32[]{:S(2)}) collective-permute-start(bf16[128,3072]{1,0:T(8,128)(2,1)S(1)} %add_convert_fusion.4), channel_id=1, source_target_pairs={{0,2},{2,4},{4,6},{6,8},{8,10},{10,12},{12,14},{1,3},{3,5},{5,7},{... | collective-permute-start | bytes 2359304 | tf_op jit(solution)/shard_map/while/body/eval_jaxpr/ppermute | solution.py:26
  99.4 16.2 %collective-permute-start = (bf16[128,3072]{1,0:T(8,128)(2,1)S(1)}, bf16[128,3072]{1,0:T(8,128)(2,1)}, u32[]{:S(2)}, u32[]{:S(2)}) collective-permute-start(bf16[128,3072]{1,0:T(8,128)(2,1)S(1)} %add_convert_fusion.4), channel_id=1, source_target_pairs={{0,2},{2,4},{4,6},{6,8},{8,10},{10,12},{12,14},{1,3},{3,5},{5,7},{... | collective-permute-start | bytes 2359304 | tf_op jit(solution)/shard_map/while/body/eval_jaxpr/ppermute | solution.py:26
  160.4 30.4 %collective-permute-start = (bf16[128,3072]{1,0:T(8,128)(2,1)S(1)}, bf16[128,3072]{1,0:T(8,128)(2,1)}, u32[]{:S(2)}, u32[]{:S(2)}) collective-permute-start(bf16[128,3072]{1,0:T(8,128)(2,1)S(1)} %add_convert_fusion.4), channel_id=1, source_target_pairs={{0,2},{2,4},{4,6},{6,8},{8,10},{10,12},{12,14},{1,3},{3,5},{5,7},{... | collective-permute-start | bytes 2359304 | tf_op jit(solution)/shard_map/while/body/eval_jaxpr/ppermute | solution.py:26
  212.7 44.0 %collective-permute-start = (bf16[128,3072]{1,0:T(8,128)(2,1)S(1)}, bf16[128,3072]{1,0:T(8,128)(2,1)}, u32[]{:S(2)}, u32[]{:S(2)}) collective-permute-start(bf16[128,3072]{1,0:T(8,128)(2,1)S(1)} %add_convert_fusion.4), channel_id=1, source_target_pairs={{0,2},{2,4},{4,6},{6,8},{8,10},{10,12},{12,14},{1,3},{3,5},{5,7},{... | collective-permute-start | bytes 2359304 | tf_op jit(solution)/shard_map/while/body/eval_jaxpr/ppermute | solution.py:26
  336.1 21.8 %collective-permute-start = (bf16[128,3072]{1,0:T(8,128)(2,1)S(1)}, bf16[128,3072]{1,0:T(8,128)(2,1)}, u32[]{:S(2)}, u32[]{:S(2)}) collective-permute-start(bf16[128,3072]{1,0:T(8,128)(2,1)S(1)} %add_convert_fusion.4), channel_id=1, source_target_pairs={{0,2},{2,4},{4,6},{6,8},{8,10},{10,12},{12,14},{1,3},{3,5},{5,7},{... | collective-permute-start | bytes 2359304 | tf_op jit(solution)/shard_map/while/body/eval_jaxpr/ppermute | solution.py:26
  384.9 26.4 %collective-permute-start = (bf16[128,3072]{1,0:T(8,128)(2,1)S(1)}, bf16[128,3072]{1,0:T(8,128)(2,1)}, u32[]{:S(2)}, u32[]{:S(2)}) collective-permute-start(bf16[128,3072]{1,0:T(8,128)(2,1)S(1)} %add_convert_fusion.4), channel_id=1, source_target_pairs={{0,2},{2,4},{4,6},{6,8},{8,10},{10,12},{12,14},{1,3},{3,5},{5,7},{... | collective-permute-start | bytes 2359304 | tf_op jit(solution)/shard_map/while/body/eval_jaxpr/ppermute | solution.py:26
  439.2 19.8 %collective-permute-start = (bf16[128,3072]{1,0:T(8,128)(2,1)S(1)}, bf16[128,3072]{1,0:T(8,128)(2,1)}, u32[]{:S(2)}, u32[]{:S(2)}) collective-permute-start(bf16[128,3072]{1,0:T(8,128)(2,1)S(1)} %add_convert_fusion.4), channel_id=1, source_target_pairs={{0,2},{2,4},{4,6},{6,8},{8,10},{10,12},{12,14},{1,3},{3,5},{5,7},{... | collective-permute-start | bytes 2359304 | tf_op jit(solution)/shard_map/while/body/eval_jaxpr/ppermute | solution.py:26
  466.1 27.4 %all-to-all-start.1 = ((bf16[2,128,3072]{2,1,0:T(8,128)(2,1)}), bf16[2,128,3072]{2,1,0:T(8,128)(2,1)}, u32[]{:S(2)}, u32[]{:S(2)}) async-start(bf16[2,128,3072]{2,1,0:T(8,128)(2,1)} %broadcast_in_dim.99), calls=%async_computation.1 | async-start | bytes 3145728 | tf_op jit(solution)/shard_map/while/body/eval_jaxpr/all_to_all | solution.py:13
  497.4 23.9 %collective-permute-start.1 = (bf16[128,3072]{1,0:T(8,128)(2,1)}, bf16[128,3072]{1,0:T(8,128)(2,1)}, u32[]{:S(2)}, u32[]{:S(2)}) collective-permute-start(bf16[128,3072]{1,0:T(8,128)(2,1)} %add_convert_fusion.5), channel_id=1, source_target_pairs={{2,0},{4,2},{6,4},{8,6},{10,8},{12,10},{14,12},{3,1},{5,3},{7,5},{... | collective-permute-start | bytes 2359304 | tf_op jit(solution)/shard_map/while/body/eval_jaxpr/ppermute | solution.py:26
  526.7 23.1 %all-to-all-start.1 = ((bf16[2,128,3072]{2,1,0:T(8,128)(2,1)}), bf16[2,128,3072]{2,1,0:T(8,128)(2,1)}, u32[]{:S(2)}, u32[]{:S(2)}) async-start(bf16[2,128,3072]{2,1,0:T(8,128)(2,1)} %broadcast_in_dim.99), calls=%async_computation.1 | async-start | bytes 3145728 | tf_op jit(solution)/shard_map/while/body/eval_jaxpr/all_to_all | solution.py:13
  553.7 17.6 %collective-permute-start.1 = (bf16[128,3072]{1,0:T(8,128)(2,1)}, bf16[128,3072]{1,0:T(8,128)(2,1)}, u32[]{:S(2)}, u32[]{:S(2)}) collective-permute-start(bf16[128,3072]{1,0:T(8,128)(2,1)} %add_convert_fusion.5), channel_id=1, source_target_pairs={{2,0},{4,2},{6,4},{8,6},{10,8},{12,10},{14,12},{3,1},{5,3},{7,5},{... | collective-permute-start | bytes 2359304 | tf_op jit(solution)/shard_map/while/body/eval_jaxpr/ppermute | solution.py:26
  576.7 29.2 %all-to-all-start.1 = ((bf16[2,128,3072]{2,1,0:T(8,128)(2,1)}), bf16[2,128,3072]{2,1,0:T(8,128)(2,1)}, u32[]{:S(2)}, u32[]{:S(2)}) async-start(bf16[2,128,3072]{2,1,0:T(8,128)(2,1)} %broadcast_in_dim.99), calls=%async_computation.1 | async-start | bytes 3145728 | tf_op jit(solution)/shard_map/while/body/eval_jaxpr/all_to_all | solution.py:13
  609.8 38.6 %collective-permute-start.1 = (bf16[128,3072]{1,0:T(8,128)(2,1)}, bf16[128,3072]{1,0:T(8,128)(2,1)}, u32[]{:S(2)}, u32[]{:S(2)}) collective-permute-start(bf16[128,3072]{1,0:T(8,128)(2,1)} %add_convert_fusion.5), channel_id=1, source_target_pairs={{2,0},{4,2},{6,4},{8,6},{10,8},{12,10},{14,12},{3,1},{5,3},{7,5},{... | collective-permute-start | bytes 2359304 | tf_op jit(solution)/shard_map/while/body/eval_jaxpr/ppermute | solution.py:26
  679.4 22.9 %all-to-all-start.1 = ((bf16[2,128,3072]{2,1,0:T(8,128)(2,1)}), bf16[2,128,3072]{2,1,0:T(8,128)(2,1)}, u32[]{:S(2)}, u32[]{:S(2)}) async-start(bf16[2,128,3072]{2,1,0:T(8,128)(2,1)} %broadcast_in_dim.99), calls=%async_computation.1 | async-start | bytes 3145728 | tf_op jit(solution)/shard_map/while/body/eval_jaxpr/all_to_all | solution.py:13
  706.2 18.7 %collective-permute-start.1 = (bf16[128,3072]{1,0:T(8,128)(2,1)}, bf16[128,3072]{1,0:T(8,128)(2,1)}, u32[]{:S(2)}, u32[]{:S(2)}) collective-permute-start(bf16[128,3072]{1,0:T(8,128)(2,1)} %add_convert_fusion.5), channel_id=1, source_target_pairs={{2,0},{4,2},{6,4},{8,6},{10,8},{12,10},{14,12},{3,1},{5,3},{7,5},{... | collective-permute-start | bytes 2359304 | tf_op jit(solution)/shard_map/while/body/eval_jaxpr/ppermute | solution.py:26
  730.2 42.1 %all-to-all-start.1 = ((bf16[2,128,3072]{2,1,0:T(8,128)(2,1)}), bf16[2,128,3072]{2,1,0:T(8,128)(2,1)}, u32[]{:S(2)}, u32[]{:S(2)}) async-start(bf16[2,128,3072]{2,1,0:T(8,128)(2,1)} %broadcast_in_dim.99), calls=%async_computation.1 | async-start | bytes 3145728 | tf_op jit(solution)/shard_map/while/body/eval_jaxpr/all_to_all | solution.py:13
  776.3 18.3 %collective-permute-start.1 = (bf16[128,3072]{1,0:T(8,128)(2,1)}, bf16[128,3072]{1,0:T(8,128)(2,1)}, u32[]{:S(2)}, u32[]{:S(2)}) collective-permute-start(bf16[128,3072]{1,0:T(8,128)(2,1)} %add_convert_fusion.5), channel_id=1, source_target_pairs={{2,0},{4,2},{6,4},{8,6},{10,8},{12,10},{14,12},{3,1},{5,3},{7,5},{... | collective-permute-start | bytes 2359304 | tf_op jit(solution)/shard_map/while/body/eval_jaxpr/ppermute | solution.py:26
  800.0 24.2 %all-to-all-start.1 = ((bf16[2,128,3072]{2,1,0:T(8,128)(2,1)}), bf16[2,128,3072]{2,1,0:T(8,128)(2,1)}, u32[]{:S(2)}, u32[]{:S(2)}) async-start(bf16[2,128,3072]{2,1,0:T(8,128)(2,1)} %broadcast_in_dim.99), calls=%async_computation.1 | async-start | bytes 3145728 | tf_op jit(solution)/shard_map/while/body/eval_jaxpr/all_to_all | solution.py:13
  828.1 16.8 %collective-permute-start.1 = (bf16[128,3072]{1,0:T(8,128)(2,1)}, bf16[128,3072]{1,0:T(8,128)(2,1)}, u32[]{:S(2)}, u32[]{:S(2)}) collective-permute-start(bf16[128,3072]{1,0:T(8,128)(2,1)} %add_convert_fusion.5), channel_id=1, source_target_pairs={{2,0},{4,2},{6,4},{8,6},{10,8},{12,10},{14,12},{3,1},{5,3},{7,5},{... | collective-permute-start | bytes 2359304 | tf_op jit(solution)/shard_map/while/body/eval_jaxpr/ppermute | solution.py:26
  850.3 24.3 %all-to-all-start.1 = ((bf16[2,128,3072]{2,1,0:T(8,128)(2,1)}), bf16[2,128,3072]{2,1,0:T(8,128)(2,1)}, u32[]{:S(2)}, u32[]{:S(2)}) async-start(bf16[2,128,3072]{2,1,0:T(8,128)(2,1)} %broadcast_in_dim.99), calls=%async_computation.1 | async-start | bytes 3145728 | tf_op jit(solution)/shard_map/while/body/eval_jaxpr/all_to_all | solution.py:13
  878.5 35.7 %collective-permute-start.1 = (bf16[128,3072]{1,0:T(8,128)(2,1)}, bf16[128,3072]{1,0:T(8,128)(2,1)}, u32[]{:S(2)}, u32[]{:S(2)}) collective-permute-start(bf16[128,3072]{1,0:T(8,128)(2,1)} %add_convert_fusion.5), channel_id=1, source_target_pairs={{2,0},{4,2},{6,4},{8,6},{10,8},{12,10},{14,12},{3,1},{5,3},{7,5},{... | collective-permute-start | bytes 2359304 | tf_op jit(solution)/shard_map/while/body/eval_jaxpr/ppermute | solution.py:26
  919.7 28.2 %all-to-all-start.1 = ((bf16[2,128,3072]{2,1,0:T(8,128)(2,1)}), bf16[2,128,3072]{2,1,0:T(8,128)(2,1)}, u32[]{:S(2)}, u32[]{:S(2)}) async-start(bf16[2,128,3072]{2,1,0:T(8,128)(2,1)} %broadcast_in_dim.99), calls=%async_computation.1 | async-start | bytes 3145728 | tf_op jit(solution)/shard_map/while/body/eval_jaxpr/all_to_all | solution.py:13
  951.8 21.3 %collective-permute-start.1 = (bf16[128,3072]{1,0:T(8,128)(2,1)}, bf16[128,3072]{1,0:T(8,128)(2,1)}, u32[]{:S(2)}, u32[]{:S(2)}) collective-permute-start(bf16[128,3072]{1,0:T(8,128)(2,1)} %add_convert_fusion.5), channel_id=1, source_target_pairs={{2,0},{4,2},{6,4},{8,6},{10,8},{12,10},{14,12},{3,1},{5,3},{7,5},{... | collective-permute-start | bytes 2359304 | tf_op jit(solution)/shard_map/while/body/eval_jaxpr/ppermute | solution.py:26
  (22 other events, 38.6 us)
Sparse Core Ops, SparseCore 0:
  973.5 187.1 all-gather.1
where the time goes:
time: 1180 us; the launch traced here: 1170 us
  waiting for transfers between devices  538 us (46%)
  blocking collectives  296 us (25%)
  starting transfers between devices  135 us (11%)
  other arithmetic  103 us (9%)
  local copies, waits for them, and re-layouts  53.4 us (5%)
  matrix products  35.5 us (3%)
  between operations  14.1 us (1%)
    all_to_all x8, blocking collectives, from_everyone(): lax.all_to_all(jnp.broadcast_to(value[None], (size, *value.shape)), axis,...  235 us
    ppermute x16, waiting for transfers between devices, from_behind(): lax.ppermute(value, axis, [(source, source + steps) for source in range(l...  227 us
    all_to_all x8, waiting for transfers between devices, from_everyone(): lax.all_to_all(jnp.broadcast_to(value[None], (size, *value.shape)), axis,...  185 us
    all_gather x1, waiting for transfers between devices, per_device(): lax.all_gather(attended, 'dp', axis=0, tiled=True)  126 us
    ppermute x16, starting transfers between devices, from_behind(): lax.ppermute(value, axis, [(source, source + steps) for source in range(l...  97.7 us
    all_to_all x1, blocking collectives, per_device(): lax.all_to_all(dproj, 'dp', split_axis=1, concat_axis=0, tiled=True)  60.1 us
    all_to_all x8, starting transfers between devices, from_everyone(): lax.all_to_all(jnp.broadcast_to(value[None], (size, *value.shape)), axis,...  36.9 us
  transfers between devices with their start and end apart: 25, of which 25 were waited for; matrix products, arithmetic and copies ran while one was open for 5% of the time, Pallas kernels for 0%

commit v1 on v0

v1 whole, which is shorter than its diff:
```python
import math
from functools import partial

import jax
import jax.numpy as jnp
from jax import lax
from jax.experimental import pallas as pl
from jax.experimental.pallas import tpu as pltpu
from jax.sharding import PartitionSpec as P

HEAD_DIM = 128
CHUNKS = 2
EPS = 1e-06
TILE = 1024
TILE_BACK = 1024
NARROW = 256
SPLIT = 2
FILL = 128
BF16 = jnp.bfloat16
F32 = jnp.float32


def nt(a, b):
    return lax.dot_general(a, b, (((1,), (1,)), ((), ())), preferred_element_type=F32)


def nn(a, b):
    rows = a.shape[0]
    if rows < FILL:
        a = jnp.concatenate([a] * (FILL // rows), axis=0)
    return jnp.dot(a, b, preferred_element_type=F32)[:rows]


def head_cols(inner):
    return [slice(h * HEAD_DIM, (h + 1) * HEAD_DIM) for h in range(inner // HEAD_DIM)]


def load_kernel(wq_in, wo_in, kv_in, mask_in, gate_in, wq, wo, kv, mask, gate, *rest):
    sems = rest[-1]
    pairs = [(wq_in, wq), (kv_in, kv), (mask_in, mask), (gate_in, gate), (wo_in, wo)]
    moves = [pltpu.make_async_copy(src, dst, sems.at[i]) for i, (src, dst) in enumerate(pairs)]
    for move in moves:
        move.start()
    for move in moves:
        move.wait()


def fetch(a, b, edge_in, av, bv, edge, chunk, sems):
    near = pltpu.make_async_copy(a, av, sems.at[0])
    far = pltpu.make_async_copy(b, bv, sems.at[1])
    own = pltpu.make_async_copy(edge_in.at[chunk], av, sems.at[0])

    @pl.when(~edge)
    def _():
        near.start()
        far.start()
        near.wait()
        far.wait()

    @pl.when(edge)
    def _():
        own.start()
        bv[...] = jnp.zeros_like(bv)
        own.wait()


def half_copies(values, share, side, chunk, own, other, sems):
    moves = []
    for which in range(2):
        mine = pl.ds(which * share, share)
        rest = pl.ds((1 - which) * share, share)
        group = [pltpu.make_async_copy(values.at[:, mine], own.at[chunk], sems.at[0])]
        if other is not None:
            group.append(pltpu.make_async_copy(values.at[:, rest], other.at[chunk], sems.at[1]))
        moves.append((side == which, group))
    return moves


def start_moves(moves):
    for wanted, group in moves:

        @pl.when(wanted)
        def _():
            for move in group:
                move.start()


def wait_moves(moves):
    for wanted, group in moves:

        @pl.when(wanted)
        def _():
            for move in group:
                move.wait()


def forward_kernel(step, sections, info, a, b, first_in, wq, wo, kv, mask, gate, *rest):
    out, xs, qr, pr, at, xh, own, other, av, bv, atv, outv, sems = rest[7:]
    rows, width = av.shape
    inner = wo.shape[0]
    share = width // 2
    heads = head_cols(inner)
    place, side = info[0], info[1]
    chunk = step - place

    @pl.when((chunk >= 0) & (chunk < CHUNKS))
    def _():
        fetch(a, b, first_in, av, bv, place == 0, chunk, sems)
        x = (av[...].astype(F32) + bv[...].astype(F32)).astype(BF16)
        xs[chunk] = x
        save_x = half_copies(xs.at[chunk], share, side, chunk, xh, None, sems.at[pl.ds(3, 2)])
        start_moves(save_x)
        xf = x.astype(F32)
        scale = lax.rsqrt(jnp.sum(xf * xf, axis=1, keepdims=True) / width + EPS)
        split = width // SPLIT

        @pl.loop(0, SPLIT)
        def _(i):
            deep = pl.ds(pl.multiple_of(i * split, split), split)
            value = nn(xs[chunk, :, deep], wq[deep, :])

            @pl.when(i == 0)
            def _():
                qr[chunk] = value

            @pl.when(i > 0)
            def _():
                qr[chunk] += value

        query = (qr[chunk] * scale).astype(BF16)
        live = mask[...] > 0
        ss = [nt(query[:, c], kv[0, :, c]) for c in heads]
        ss = [jnp.where(live, s * (1 / math.sqrt(HEAD_DIM)), -1e30) for s in ss]
        es = [jnp.exp(s - jnp.max(s, axis=1, keepdims=True)) for s in ss]
        ps = [e * (1 / jnp.sum(e, axis=1, keepdims=True)) for e in es]
        os = [nn(p.astype(BF16), kv[1, :, c]).astype(BF16) for p, c in zip(ps, heads)]
        for p, o, c in zip(ps, os, heads):
            pr[chunk, :, c] = p
            atv[:, c] = o
        save_a = pltpu.make_async_copy(atv, at.at[chunk], sems.at[5])
        save_a.start()
        lead = (1 - side).astype(F32)

        @pl.loop(0, width // TILE)
        def _(i):
            cols = pl.ds(pl.multiple_of(i * TILE, TILE), TILE)
            proj = nn(atv[...], wo[:, cols])
            outv[:, cols] = (lead * xs[chunk, :, cols].astype(F32) + gate[:, cols] * proj).astype(BF16)

        send = pltpu.make_async_copy(outv, out, sems.at[2])
        send.start()
        if step >= sections - 1:
            final = half_copies(outv, share, side, chunk, own, other, sems.at[pl.ds(6, 2)])

            @pl.when(place == sections - 1)
            def _():
                start_moves(final)
                wait_moves(final)

        save_a.wait()
        wait_moves(save_x)
        send.wait()


def backward_kernel(step, sections, info, a, b, last_in, wq, wo, kv, gate, *rest):
    out, xs, qr, pr, dp, dyh, own, other, av, bv, dpv, dav, dqv, outv, sems = rest[7:]
    rows, width = av.shape
    inner = wo.shape[0]
    share = width // 2
    heads = head_cols(inner)
    place, side = info[0], info[1]
    chunk = step - (sections - 1 - place)

    @pl.when((chunk >= 0) & (chunk < CHUNKS))
    def _():
        fetch(a, b, last_in, av, bv, place == sections - 1, chunk, sems)
        grad = (av[...].astype(F32) + bv[...].astype(F32)).astype(BF16)
        av[...] = grad
        dpv[...] = (gate[...] * grad.astype(F32)).astype(BF16)
        save_p = pltpu.make_async_copy(dpv, dp.at[chunk], sems.at[5])
        save_p.start()
        save_y = half_copies(av, share, side, chunk, dyh, None, sems.at[pl.ds(3, 2)])
        start_moves(save_y)

        @pl.loop(0, inner // NARROW)
        def _(i):
            cols = pl.ds(pl.multiple_of(i * NARROW, NARROW), NARROW)
            dav[:, cols] = nt(dpv[...], wo[cols, :]).astype(BF16)

        dprobs = [nt(dav[:, c], kv[1, :, c]) for c in heads]
        ps = [pr[chunk, :, c] for c in heads]
        rs = [jnp.sum(p * d, axis=1, keepdims=True) for p, d in zip(ps, dprobs)]
        ds = [(p * (d - r)).astype(BF16) for p, d, r in zip(ps, dprobs, rs)]
        dqs = [(nn(d, kv[0, :, c]) * (1 / math.sqrt(HEAD_DIM))).astype(BF16) for d, c in zip(ds, heads)]
        total = jnp.zeros((rows, HEAD_DIM), F32)
        for dq, c in zip(dqs, heads):
            dqv[:, c] = dq
            total = total + dq.astype(F32) * qr[chunk, :, c]
        mean = jnp.sum(total, axis=1, keepdims=True) / width
        xf = xs[chunk].astype(F32)
        scale = lax.rsqrt(jnp.sum(xf * xf, axis=1, keepdims=True) / width + EPS)
        coeff = scale * scale * mean
        lead = (1 - side).astype(F32)

        @pl.loop(0, width // TILE_BACK)
        def _(i):
            cols = pl.ds(pl.multiple_of(i * TILE_BACK, TILE_BACK), TILE_BACK)
            dn = nt(dqv[...], wq[cols, :])
            piece = scale * (dn - xs[chunk, :, cols].astype(F32) * coeff)
            outv[:, cols] = (lead * av[:, cols].astype(F32) + piece).astype(BF16)

        send = pltpu.make_async_copy(outv, out, sems.at[2])
        send.start()
        if step >= sections - 1:
            final = half_copies(outv, share, side, chunk, own, other, sems.at[pl.ds(6, 2)])

            @pl.when(place == 0)
            def _():
                start_moves(final)
                wait_moves(final)

        save_p.wait()
        wait_moves(save_y)
        send.wait()


ANY = pl.BlockSpec(memory_space=pl.ANY)
SMEM = pl.BlockSpec(memory_space=pltpu.SMEM)
VMEM = pl.BlockSpec(memory_space=pltpu.VMEM)
LIMIT = 16 << 20


def held(x):
    return pltpu.VMEM(x.shape, x.dtype)


def run_load(fixed, typed, free):
    return pl.pallas_call(
        load_kernel,
        out_shape=(*map(held, fixed), *typed, *free),
        in_specs=[ANY] * 5,
        out_specs=(VMEM,) * (5 + len(typed)) + (ANY,) * len(free),
        scratch_shapes=[pltpu.SemaphoreType.DMA((5,))],
        compiler_params=pltpu.CompilerParams(vmem_limit_bytes=LIMIT),
        name="load_weights",
    )(*fixed)


def run_step(kernel, name, step, sections, info, a, b, edge_in, fixed, typed, free, scratch):
    rows, width = a.shape
    lead = 4 + len(fixed)
    state = (*typed, *free)
    like = jax.ShapeDtypeStruct((rows, width), BF16)
    return pl.pallas_call(
        partial(kernel, step, sections),
        out_shape=(like, *map(held, typed), *[jax.ShapeDtypeStruct(x.shape, x.dtype) for x in free]),
        in_specs=[SMEM] + [ANY] * 3 + [VMEM] * (len(fixed) + len(typed)) + [ANY] * len(free),
        out_specs=(ANY,) + (VMEM,) * len(typed) + (ANY,) * len(free),
        scratch_shapes=[pltpu.VMEM((rows, width), BF16)] * 2 + scratch
        + [pltpu.VMEM((rows, width), BF16), pltpu.SemaphoreType.DMA((8,))],
        input_output_aliases={lead + i: 1 + i for i in range(len(state))},
        compiler_params=pltpu.CompilerParams(vmem_limit_bytes=LIMIT),
        name=name,
    )(info, a, b, edge_in, *fixed, *state)


def per_device(latents, caption_kv, caption_mask, query_weight, out_weight, gate, cotangent):
    _, micro, tok, width = latents.shape
    rows = micro * tok // CHUNKS
    inner = out_weight.shape[1]
    sections = lax.axis_size("pipe")
    sides = lax.axis_size("mp")
    replicas = lax.axis_size("dp")
    pos = lax.axis_index("pipe")
    side = lax.axis_index("mp")
    share = width // sides
    start = latents.reshape(CHUNKS, rows, width)
    cot = cotangent.reshape(CHUNKS, rows, width)
    axes = ("pipe", "mp")
    info = jnp.stack([pos, side]).astype(jnp.int32)

    def spot(p, m):
        return p * sides + m

    def shift(value, sources, step, swap):
        pairs = [(spot(p, m), spot(p + step, (1 - m) if swap else m)) for p in sources for m in range(sides)]
        return lax.ppermute(value, axes, pairs)

    def swap_sides(value, p):
        return lax.ppermute(value, axes, [(spot(p, m), spot(p, 1 - m)) for m in range(sides)])

    full = ((CHUNKS, rows, width), BF16)
    mid = ((CHUNKS, rows, inner), F32)
    narrow = ((CHUNKS, rows, inner), BF16)
    part = ((CHUNKS, rows, share), BF16)
    weights = (query_weight[0], out_weight[0], caption_kv[0, 0], caption_mask, gate)
    free = [narrow, part, part, part, full, part, part, part, ((rows, width), BF16)]
    wq, wo, kv, live, gain, xs, qr, pr, *loaded = run_load(
        weights, [pltpu.VMEM(*x) for x in (full, mid, mid)], [jax.ShapeDtypeStruct(*x) for x in free]
    )
    shared, ahead, behind = [xs, qr, pr], loaded[:4], loaded[4:8]
    ahead_scratch = [pltpu.VMEM((rows, inner), BF16)]
    behind_scratch = [pltpu.VMEM((rows, width), BF16)] + [pltpu.VMEM((rows, inner), BF16)] * 2
    turns = sections + CHUNKS - 1
    a = b = c = d = loaded[8]
    for t in range(sections - 1 + turns):
        f = t
        if f < turns:
            out, *state = run_step(
                forward_kernel, "section_forward", f, sections, info, a, b, start,
                (wq, wo, kv, live, gain), shared, ahead, ahead_scratch,
            )
            shared, ahead = state[:3], state[3:]
            sources = [p for p in range(sections - 1) if 0 <= f - p < CHUNKS]
            if sources:
                a = shift(out, sources, 1, False)
                b = shift(out, sources, 1, True)
        g = t - (sections - 1)
        if 0 <= g < turns:
            if g == CHUNKS:
                attended, again = lax.optimization_barrier((ahead[0], (weights, out)))
                everyone = lax.all_gather(attended.reshape(CHUNKS * rows, inner), "dp", axis=0, tiled=True)
                wq, wo, kv, live, gain = run_load(again[0], [], [])
            out, *state = run_step(
                backward_kernel, "section_backward", g, sections, info, c, d, cot,
                (wq, wo, kv, gain), shared, behind, behind_scratch,
            )
            shared, behind = state[:3], state[3:]
            sources = [p for p in range(1, sections) if 0 <= g - (sections - 1 - p) < CHUNKS]
            if sources:
                c = shift(out, sources, -1, False)
                d = shift(out, sources, -1, True)
    _, xh, last, last_other = ahead
    dp, dyh, low, low_other = behind
    pos, _ = lax.optimization_barrier((pos, out))

    from_next = shift(xh, list(range(1, sections)), -1, False)
    last_theirs = swap_sides(last_other, sections - 1)
    from_before = shift(dyh, list(range(sections - 1)), 1, False)
    low_theirs = swap_sides(low_other, 0)

    def total(mine, theirs):
        return (mine.astype(F32) + theirs.astype(F32)).astype(BF16)

    section_out = jnp.where(pos == sections - 1, total(last, last_theirs), from_next)
    input_grad = jnp.where(pos == 0, total(low, low_theirs), from_before)

    columns = dp.reshape(CHUNKS * rows, width).T.reshape(replicas, width // replicas, CHUNKS * rows)
    columns = lax.all_to_all(columns, "dp", split_axis=0, concat_axis=0, tiled=True)
    weight_grad = jnp.einsum(
        "srk,sdr->kd", everyone.reshape(replicas, CHUNKS * rows, inner), columns, preferred_element_type=F32
    )
    return (
        section_out.reshape(1, 1, micro, tok, share),
        input_grad.reshape(1, 1, micro, tok, share),
        weight_grad[None],
    )


def solution(mesh):
    return jax.shard_map(
        per_device,
        mesh=mesh,
        in_specs=(
            P("dp", None, None, None),
            P("dp", "pipe", None, None, "mp"),
            P("dp", None),
            P("pipe", None, "mp"),
            P("pipe", "mp", None),
            P("pipe", None),
            P("dp", None, None, None),
        ),
        out_specs=(
            P("pipe", "dp", None, None, "mp"),
            P("pipe", "dp", None, None, "mp"),
            P("pipe", "mp", "dp"),
        ),
        check_vma=False,
    )
```

time: 1180 us -> 364 us (0.31)
  the two profiles are of different devices: /device:TPU:16 before, /device:TPU:2 now
where the time goes in v1:
time: 364 us; the launch traced here: 363 us
  waiting for transfers between devices  210 us (58%)
  starting transfers between devices  78.6 us (22%)
  Pallas kernels  32 us (9%)
  local copies, waits for them, and re-layouts  18.8 us (5%)
  between operations  14.8 us (4%)
  matrix products  6.1 us (2%)
    ppermute x34, waiting for transfers between devices, shift(): return lax.ppermute(value, axes, pairs)  203 us
    ppermute x34, starting transfers between devices, shift(): return lax.ppermute(value, axes, pairs)  52 us
    pallas_call x18, Pallas kernels, run_step(): pl.pallas_call(partial(kernel, step, sections), out_shape=(like, *map(hel...  29.7 us
    all_to_all x1, starting transfers between devices, per_device(): lax.all_to_all(columns, 'dp', split_axis=0, concat_axis=0, tiled=True)  18.5 us
    unnamed x46, local copies, waits for them, and re-layouts  17.6 us
    ppermute x2, starting transfers between devices, swap_sides(): lax.ppermute(value, axes, [(spot(p, m), spot(p, 1 - m)) for m in range(si...  8.09 us
  transfers between devices with their start and end apart: 38, of which 7 were waited for; matrix products, arithmetic and copies ran while one was open for 1% of the time, Pallas kernels for 5%

profile of v1, /device:TPU:2, one launch (start us, length us, event | category | flops | bytes accessed | tf_op | source)
XLA Modules:
  0.0 362.8 jit_solution(11324480221780605388)
XLA Ops:
  7.3 2.3 copy-done.12
  9.6 2.3 copy-done.14
  15.5 4.1 %section_forward.9 = (bf16[64,3072]{1,0:T(8,128)(2,1)S(1)}, bf16[2,64,3072]{2,1,0:T(8,128)(2,1)S(1)}, f32[2,64,768]{2,1,0:T(8,128)S(1)}, f32[2,64,768]{2,1,0:T(8...) custom-call(s32[2]{0:T(128)S(1)} %pad_add_fusion.info, ...), custom_call_target="tpu_custom_call", output_to_operand_aliasing={{1}: (9, {}), {2}: (10, {}), {3}: (11, {}), {4}: (12, {}), ... | custom-call | tf_op jit(solution)/shard_map/section_forward/pallas_call | solution.py:254
  20.9 3.7 %collective-permute-start.1 = (bf16[64,3072]{1,0:T(8,128)(2,1)S(1)}, bf16[64,3072]{1,0:T(8,128)(2,1)S(1)}, u32[]{:S(2)}, u32[]{:S(2)}) collective-permute-start(bf16[64,3072]{1,0:T(8,128)(2,1)S(1)} %get-tuple-element.182), channel_id=1, source_target_pairs={{0,3},{1,2},{16,19},{17,18},{32,35},{33,34},{48,51},{49,50},{64,67... | collective-permute-start | bytes 1179656 | tf_op jit(solution)/shard_map/ppermute | solution.py:287
  24.6 5.2 %collective-permute-done.1.b = bf16[64,3072]{1,0:T(8,128)(2,1)S(1)} collective-permute-done((bf16[64,3072]{1,0:T(8,128)(2,1)S(1)}, bf16[64,3072]{1,0:T(8,128)(2,1)S(1)}, u32[]{:S(2)}, u32[]{:S(2)}) %collective-permute-start.1) | collective-permute-done | bytes 393248 | tf_op jit(solution)/shard_map/ppermute | solution.py:287
  29.8 4.1 %section_forward.10 = (bf16[64,3072]{1,0:T(8,128)(2,1)S(1)}, bf16[2,64,3072]{2,1,0:T(8,128)(2,1)S(1)}, f32[2,64,768]{2,1,0:T(8,128)S(1)}, f32[2,64,768]{2,1,0:T(...) custom-call(s32[2]{0:T(128)S(1)} %pad_add_fusion.info, ...), custom_call_target="tpu_custom_call", output_to_operand_aliasing={{1}: (9, {}), {2}: (10, {}), {3}: (11, {}), {4}: (12, {}), ... | custom-call | tf_op jit(solution)/shard_map/section_forward/pallas_call | solution.py:254
  34.0 5.9 %collective-permute-start.2 = (bf16[64,3072]{1,0:T(8,128)(2,1)S(1)}, bf16[64,3072]{1,0:T(8,128)(2,1)S(1)}, u32[]{:S(2)}, u32[]{:S(2)}) collective-permute-start(bf16[64,3072]{1,0:T(8,128)(2,1)S(1)} %get-tuple-element.190), channel_id=1, source_target_pairs={{0,2},{1,3},{2,4},{3,5},{16,18},{17,19},{18,20},{19,21},{32,34},{3... | collective-permute-start | bytes 1179656 | tf_op jit(solution)/shard_map/ppermute | solution.py:287
  39.8 4.0 %collective-permute-start.3 = (bf16[64,3072]{1,0:T(8,128)(2,1)S(1)}, bf16[64,3072]{1,0:T(8,128)(2,1)S(1)}, u32[]{:S(2)}, u32[]{:S(2)}) collective-permute-start(bf16[64,3072]{1,0:T(8,128)(2,1)S(1)} %get-tuple-element.190), channel_id=1, source_target_pairs={{0,3},{1,2},{2,5},{3,4},{16,19},{17,18},{18,21},{19,20},{32,35},{3... | collective-permute-start | bytes 1179656 | tf_op jit(solution)/shard_map/ppermute | solution.py:287
  43.9 5.2 %collective-permute-done.3.b = bf16[64,3072]{1,0:T(8,128)(2,1)S(1)} collective-permute-done((bf16[64,3072]{1,0:T(8,128)(2,1)S(1)}, bf16[64,3072]{1,0:T(8,128)(2,1)S(1)}, u32[]{:S(2)}, u32[]{:S(2)}) %collective-permute-start.3) | collective-permute-done | bytes 393248 | tf_op jit(solution)/shard_map/ppermute | solution.py:287
  69.2 2.3 copy-done.13
  71.5 2.3 copy-done.15
  75.5 1.5 load_weights.3
  88.4 171.1 %collective-permute-done.30.a = bf16[64,3072]{1,0:T(8,128)(2,1)S(1)} collective-permute-done((bf16[64,3072]{1,0:T(8,128)(2,1)S(1)}, bf16[64,3072]{1,0:T(8,128)(2,1)S(1)}, u32[]{:S(2)}, u32[]{:S(2)}) %collective-permute-start.30) | collective-permute-done | bytes 393248 | tf_op jit(solution)/shard_map/ppermute | solution.py:287
  259.5 9.8 %collective-permute-done.31.b = bf16[64,3072]{1,0:T(8,128)(2,1)S(1)} collective-permute-done((bf16[64,3072]{1,0:T(8,128)(2,1)S(1)}, bf16[64,3072]{1,0:T(8,128)(2,1)S(1)}, u32[]{:S(2)}, u32[]{:S(2)}) %collective-permute-start.31) | collective-permute-done | bytes 393248 | tf_op jit(solution)/shard_map/ppermute | solution.py:287
  269.3 6.1 %section_backward.16 = (bf16[64,3072]{1,0:T(8,128)(2,1)S(1)}, bf16[2,64,3072]{2,1,0:T(8,128)(2,1)S(1)}, f32[2,64,768]{2,1,0:T(8,128)S(1)}, f32[2,64,768]{2,1,0:T...) custom-call(s32[2]{0:T(128)S(1)} %pad_add_fusion.info, ...), custom_call_target="tpu_custom_call", output_to_operand_aliasing={{1}: (8, {}), {2}: (9, {}), {3}: (10, {}), {4}: (11, {}), {... | custom-call | tf_op jit(solution)/shard_map/section_backward/pallas_call | solution.py:254
  278.0 3.8 %collective-permute-done.32.a = bf16[64,3072]{1,0:T(8,128)(2,1)S(1)} collective-permute-done((bf16[64,3072]{1,0:T(8,128)(2,1)S(1)}, bf16[64,3072]{1,0:T(8,128)(2,1)S(1)}, u32[]{:S(2)}, u32[]{:S(2)}) %collective-permute-start.32) | collective-permute-done | bytes 393248 | tf_op jit(solution)/shard_map/ppermute | solution.py:287
  281.8 7.9 %collective-permute-done.33.b = bf16[64,3072]{1,0:T(8,128)(2,1)S(1)} collective-permute-done((bf16[64,3072]{1,0:T(8,128)(2,1)S(1)}, bf16[64,3072]{1,0:T(8,128)(2,1)S(1)}, u32[]{:S(2)}, u32[]{:S(2)}) %collective-permute-start.33) | collective-permute-done | bytes 393248 | tf_op jit(solution)/shard_map/ppermute | solution.py:287
  289.7 6.3 %section_backward.17 = (bf16[64,3072]{1,0:T(8,128)(2,1)}, bf16[2,64,3072]{2,1,0:T(8,128)(2,1)S(1)}, f32[2,64,768]{2,1,0:T(8,128)S(1)}, f32[2,64,768]{2,1,0:T(8,1...) custom-call(s32[2]{0:T(128)S(1)} %pad_add_fusion.info, ...), custom_call_target="tpu_custom_call", output_to_operand_aliasing={{1}: (8, {}), {2}: (9, {}), {3}: (10, {}), {4}: (11, {}), {... | custom-call | tf_op jit(solution)/shard_map/section_backward/pallas_call | solution.py:254
  298.7 18.5 %all-to-all-start = ((bf16[48,64,128]{2,1,0:T(8,128)(2,1)}), bf16[48,64,128]{2,1,0:T(8,128)(2,1)S(1)}, u32[]{:S(2)}, u32[]{:S(2)}) async-start(bf16[48,64,128]{2,1,0:T(8,128)(2,1)} %bitcast.13), calls=%async_computation | async-start | bytes 1572864 | tf_op jit(solution)/shard_map/all_to_all | solution.py:349
  317.9 14.1 %collective-permute-start.17 = (bf16[2,64,1536]{2,1,0:T(8,128)(2,1)}, bf16[2,64,1536]{2,1,0:T(8,128)(2,1)S(1)}, u32[]{:S(2)}, u32[]{:S(2)}) collective-permute-start(bf16[2,64,1536]{2,1,0:T(8,128)(2,1)} %copy-done.9), channel_id=1, source_target_pairs={{2,0},{3,1},{4,2},{5,3},{6,4},{7,5},{8,6},{9,7},{10,8},{11,9},{12,... | collective-permute-start | bytes 1179656 | tf_op jit(solution)/shard_map/ppermute | solution.py:287
  332.0 7.4 %collective-permute-start.34 = (bf16[2,64,1536]{2,1,0:T(8,128)(2,1)}, bf16[2,64,1536]{2,1,0:T(8,128)(2,1)S(1)}, u32[]{:S(2)}, u32[]{:S(2)}) collective-permute-start(bf16[2,64,1536]{2,1,0:T(8,128)(2,1)} %copy-done.8), channel_id=1, source_target_pairs={{0,1},{1,0},{16,17},{17,16},{32,33},{33,32},{48,49},{49,48},{64,65... | collective-permute-start | bytes 1179656 | tf_op jit(solution)/shard_map/ppermute | solution.py:290
  340.7 1.9 fusion.1
  342.6 6.4 %collective-permute-done.34 = bf16[2,64,1536]{2,1,0:T(8,128)(2,1)S(1)} collective-permute-done((bf16[2,64,1536]{2,1,0:T(8,128)(2,1)}, bf16[2,64,1536]{2,1,0:T(8,128)(2,1)S(1)}, u32[]{:S(2)}, u32[]{:S(2)}) %collective-permute-start.34) | collective-permute-done | bytes 393248 | tf_op jit(solution)/shard_map/ppermute | solution.py:290
  349.9 6.1 %convolution_bitcast_fusion = f32[1,768,64]{1,2,0:T(8,128)} fusion(bf16[48,64,128]{2,1,0:T(8,128)(2,1)S(1)} %all-to-all-done, bf16[48,128,768]{2,1,0:T(8,128)(2,1)} %bitcast.48), kind=kOutput, calls=%fused_computation | convolution fusion | flops 603979776 | bytes 10420224 | tf_op jit(solution)/shard_map/srk,sdr->kd/dot_general | solution.py:350
  (124 shorter events, 45.6 us)
Async XLA Ops:
  7.2 342.7 %all-gather.2.cloned.1.call-start = ((), (), s32[]{:S(2)}) async-start(), calls=%async_computation.1 | async-start | bytes 9633792 | tf_op jit(solution)/shard_map/all_gather | solution.py:322
  19.6 5.0 %collective-permute-start = (bf16[64,3072]{1,0:T(8,128)(2,1)S(1)}, bf16[64,3072]{1,0:T(8,128)(2,1)S(1)}, u32[]{:S(2)}, u32[]{:S(2)}) collective-permute-start(bf16[64,3072]{1,0:T(8,128)(2,1)S(1)} %get-tuple-element.182), channel_id=1, source_target_pairs={{0,2},{1,3},{16,18},{17,19},{32,34},{33,35},{48,50},{49,51},{64,66... | collective-permute-start | bytes 1179656 | tf_op jit(solution)/shard_map/ppermute | solution.py:287
  20.9 8.9 %collective-permute-start.1 = (bf16[64,3072]{1,0:T(8,128)(2,1)S(1)}, bf16[64,3072]{1,0:T(8,128)(2,1)S(1)}, u32[]{:S(2)}, u32[]{:S(2)}) collective-permute-start(bf16[64,3072]{1,0:T(8,128)(2,1)S(1)} %get-tuple-element.182), channel_id=1, source_target_pairs={{0,3},{1,2},{16,19},{17,18},{32,35},{33,34},{48,51},{49,50},{64,67... | collective-permute-start | bytes 1179656 | tf_op jit(solution)/shard_map/ppermute | solution.py:287
  34.0 9.9 %collective-permute-start.2 = (bf16[64,3072]{1,0:T(8,128)(2,1)S(1)}, bf16[64,3072]{1,0:T(8,128)(2,1)S(1)}, u32[]{:S(2)}, u32[]{:S(2)}) collective-permute-start(bf16[64,3072]{1,0:T(8,128)(2,1)S(1)} %get-tuple-element.190), channel_id=1, source_target_pairs={{0,2},{1,3},{2,4},{3,5},{16,18},{17,19},{18,20},{19,21},{32,34},{3... | collective-permute-start | bytes 1179656 | tf_op jit(solution)/shard_map/ppermute | solution.py:287
  39.8 9.3 %collective-permute-start.3 = (bf16[64,3072]{1,0:T(8,128)(2,1)S(1)}, bf16[64,3072]{1,0:T(8,128)(2,1)S(1)}, u32[]{:S(2)}, u32[]{:S(2)}) collective-permute-start(bf16[64,3072]{1,0:T(8,128)(2,1)S(1)} %get-tuple-element.190), channel_id=1, source_target_pairs={{0,3},{1,2},{2,5},{3,4},{16,19},{17,18},{18,21},{19,20},{32,35},{3... | collective-permute-start | bytes 1179656 | tf_op jit(solution)/shard_map/ppermute | solution.py:287
  49.7 1.4 collective-permute-start.4
  51.8 1.4 collective-permute-start.6
  53.8 1.4 collective-permute-start.8
  55.9 1.4 collective-permute-start.10
  60.2 3.4 collective-permute-start.14
  60.9 2.7 collective-permute-start.15
  62.2 2.1 collective-permute-start.18
  62.9 1.4 collective-permute-start.19
  67.6 9.3 %collective-permute-start.20 = (bf16[64,3072]{1,0:T(8,128)(2,1)}, bf16[64,3072]{1,0:T(8,128)(2,1)S(1)}, u32[]{:S(2)}, u32[]{:S(2)}) collective-permute-start(bf16[64,3072]{1,0:T(8,128)(2,1)} %copy-done.22), channel_id=1, source_target_pairs={{12,10},{13,11},{14,12},{15,13},{28,26},{29,27},{30,28},{31,29},{4... | collective-permute-start | bytes 1179656 | tf_op jit(solution)/shard_map/ppermute | solution.py:287
  68.4 8.5 %collective-permute-start.21 = (bf16[64,3072]{1,0:T(8,128)(2,1)}, bf16[64,3072]{1,0:T(8,128)(2,1)S(1)}, u32[]{:S(2)}, u32[]{:S(2)}) collective-permute-start(bf16[64,3072]{1,0:T(8,128)(2,1)} %copy-done.22), channel_id=1, source_target_pairs={{12,11},{13,10},{14,13},{15,12},{28,27},{29,26},{30,29},{31,28},{4... | collective-permute-start | bytes 1179656 | tf_op jit(solution)/shard_map/ppermute | solution.py:287
  85.8 173.7 %collective-permute-start.30 = (bf16[64,3072]{1,0:T(8,128)(2,1)S(1)}, bf16[64,3072]{1,0:T(8,128)(2,1)S(1)}, u32[]{:S(2)}, u32[]{:S(2)}) collective-permute-start(bf16[64,3072]{1,0:T(8,128)(2,1)S(1)} %get-tuple-element.314), channel_id=1, source_target_pairs={{2,0},{3,1},{4,2},{5,3},{18,16},{19,17},{20,18},{21,19},{34,32},{3... | collective-permute-start | bytes 1179656 | tf_op jit(solution)/shard_map/ppermute | solution.py:287
  87.1 182.2 %collective-permute-start.31 = (bf16[64,3072]{1,0:T(8,128)(2,1)S(1)}, bf16[64,3072]{1,0:T(8,128)(2,1)S(1)}, u32[]{:S(2)}, u32[]{:S(2)}) collective-permute-start(bf16[64,3072]{1,0:T(8,128)(2,1)S(1)} %get-tuple-element.314), channel_id=1, source_target_pairs={{2,1},{3,0},{4,3},{5,2},{18,17},{19,16},{20,19},{21,18},{34,33},{3... | collective-permute-start | bytes 1179656 | tf_op jit(solution)/shard_map/ppermute | solution.py:287
  275.4 6.4 %collective-permute-start.32 = (bf16[64,3072]{1,0:T(8,128)(2,1)S(1)}, bf16[64,3072]{1,0:T(8,128)(2,1)S(1)}, u32[]{:S(2)}, u32[]{:S(2)}) collective-permute-start(bf16[64,3072]{1,0:T(8,128)(2,1)S(1)} %get-tuple-element.322), channel_id=1, source_target_pairs={{2,0},{3,1},{18,16},{19,17},{34,32},{35,33},{50,48},{51,49},{66,64... | collective-permute-start | bytes 1179656 | tf_op jit(solution)/shard_map/ppermute | solution.py:287
  276.7 13.0 %collective-permute-start.33 = (bf16[64,3072]{1,0:T(8,128)(2,1)S(1)}, bf16[64,3072]{1,0:T(8,128)(2,1)S(1)}, u32[]{:S(2)}, u32[]{:S(2)}) collective-permute-start(bf16[64,3072]{1,0:T(8,128)(2,1)S(1)} %get-tuple-element.322), channel_id=1, source_target_pairs={{2,1},{3,0},{18,17},{19,16},{34,33},{35,32},{50,49},{51,48},{66,65... | collective-permute-start | bytes 1179656 | tf_op jit(solution)/shard_map/ppermute | solution.py:287
  298.7 51.1 %all-to-all-start = ((bf16[48,64,128]{2,1,0:T(8,128)(2,1)}), bf16[48,64,128]{2,1,0:T(8,128)(2,1)S(1)}, u32[]{:S(2)}, u32[]{:S(2)}) async-start(bf16[48,64,128]{2,1,0:T(8,128)(2,1)} %bitcast.13), calls=%async_computation | async-start | bytes 1572864 | tf_op jit(solution)/shard_map/all_to_all | solution.py:349
  317.2 23.5 %collective-permute-start.16 = (bf16[2,64,1536]{2,1,0:T(8,128)(2,1)}, bf16[2,64,1536]{2,1,0:T(8,128)(2,1)S(1)}, u32[]{:S(2)}, u32[]{:S(2)}) collective-permute-start(bf16[2,64,1536]{2,1,0:T(8,128)(2,1)} %copy-done.10), channel_id=1, source_target_pairs={{14,15},{15,14},{30,31},{31,30},{46,47},{47,46},{62,63},{63,62},{7... | collective-permute-start | bytes 1179656 | tf_op jit(solution)/shard_map/ppermute | solution.py:290
  317.9 22.8 %collective-permute-start.17 = (bf16[2,64,1536]{2,1,0:T(8,128)(2,1)}, bf16[2,64,1536]{2,1,0:T(8,128)(2,1)S(1)}, u32[]{:S(2)}, u32[]{:S(2)}) collective-permute-start(bf16[2,64,1536]{2,1,0:T(8,128)(2,1)} %copy-done.9), channel_id=1, source_target_pairs={{2,0},{3,1},{4,2},{5,3},{6,4},{7,5},{8,6},{9,7},{10,8},{11,9},{12,... | collective-permute-start | bytes 1179656 | tf_op jit(solution)/shard_map/ppermute | solution.py:287
  332.0 17.0 %collective-permute-start.34 = (bf16[2,64,1536]{2,1,0:T(8,128)(2,1)}, bf16[2,64,1536]{2,1,0:T(8,128)(2,1)S(1)}, u32[]{:S(2)}, u32[]{:S(2)}) collective-permute-start(bf16[2,64,1536]{2,1,0:T(8,128)(2,1)} %copy-done.8), channel_id=1, source_target_pairs={{0,1},{1,0},{16,17},{17,16},{32,33},{33,32},{48,49},{49,48},{64,65... | collective-permute-start | bytes 1179656 | tf_op jit(solution)/shard_map/ppermute | solution.py:290
  339.4 9.6 %collective-permute-start.35 = (bf16[2,64,1536]{2,1,0:T(8,128)(2,1)}, bf16[2,64,1536]{2,1,0:T(8,128)(2,1)S(1)}, u32[]{:S(2)}, u32[]{:S(2)}) collective-permute-start(bf16[2,64,1536]{2,1,0:T(8,128)(2,1)} %copy-done.5), channel_id=1, source_target_pairs={{0,2},{1,3},{2,4},{3,5},{4,6},{5,7},{6,8},{7,9},{8,10},{9,11},{10,... | collective-permute-start | bytes 1179656 | tf_op jit(solution)/shard_map/ppermute | solution.py:287
  (37 other events, 60.9 us)
Sparse Core Ops, SparseCore 0:
  67.7 239.1 all-gather.1
